TPU v7x, 32 devices: a whole 2x2x4 slice. The times are simulated.
32 devices in a mesh: dp: 2 (over core), expert: 16 (over z, y, x).
Axes of the slice: x: 2, y: 2, z: 4, core: 2. Of those that a mesh axis runs over, the one named last changes fastest.
Arguments:
- tokens: bfloat16 [4096, 1152], P(('dp', 'expert')), may hold values from -6 to 6
- out_grad: bfloat16 [4096, 1152], P(('dp', 'expert')), may hold values from -6 to 6
- gates: float32 [4096, 2], P(('dp', 'expert')), may hold values from 0.05 to 1
- expert_ids: int32 [4096, 2], P(('dp', 'expert')), may hold values from 0 to 15, all different within a row; in each aligned block of 128 rows (0 to 127, 128 to 255, ...) at most 24 rows name the same one
- swap_list: int32 [16], replicated, may hold values from 0 to 15, as said below
- w_in: bfloat16 [16, 1152, 3072], P('expert', None, 'dp'), may hold values from -0.1875 to 0.1875
- w_out: bfloat16 [16, 3072, 1152], P('expert', 'dp'), may hold values from -0.109375 to 0.109375
- first_moment: float32 [16, 1152, 3072], P('expert', None, 'dp'), may hold values from -12 to 12
- second_moment: float32 [16, 1152, 3072], P('expert', None, 'dp'), may hold values from 1 to 100
Outputs:
- x_grad: bfloat16 [4096, 1152], P(('dp', 'expert'))
- adam_out: bfloat16 [16, 1152, 3072], P('expert', None, 'dp')
Inputs may be any that keep to these rules, and one draw needn't show every extreme that they name: `expert_ids`: among the 128 tokens of one device no expert is named by more than 24 rows; a token's two experts differ. swap_list[e] is e or e XOR 16/2, and swap_list[swap_list[e]] = e; swap_list[0] = 8 and swap_list[15] = 7.
All inputs are finite; a program needn't handle non-finite values.
Results may differ from a plain program's by a relative error of at most 0.015.
Values may be sent and summed in bfloat16 or wider, within the bound.
No kernel may reach another device: no remote copies, remote signals or barrier semaphores. Data moves between devices by JAX's collectives and lax.ppermute only.
A program may use at most 128 MiB of HBM per device.

v0:
```python
import jax
import jax.numpy as jnp
from jax import lax
from jax.sharding import PartitionSpec as P

ADAM_STEP = 100
coef_c = 0.7978845608028654
coef_a = 0.044715
beta_one = 0.9
beta_two = 0.999
adam_eps = 1e-08


def partner(block, axis, apart):
    count = lax.axis_size(axis)
    route = []
    for low in range(count):
        high = low | 1 << apart
        if high != low and high < count:
            route += [(low, high), (high, low)]
    return lax.ppermute(block, axis, route)


def gelu_slope(pre_act):
    inner_arg = coef_c * (pre_act + coef_a * pre_act * pre_act * pre_act)
    tanh_val = jnp.tanh(inner_arg)
    return 0.5 * (1.0 + tanh_val) + 0.5 * pre_act * (1.0 - tanh_val * tanh_val) * coef_c * (
        1.0 + 3.0 * coef_a * pre_act * pre_act
    )


def pack_rows(id_block, x_block, g_block, dest_table, capacity):
    expert_count = dest_table.shape[0]
    flat_ids = id_block.reshape(-1)
    assigned = flat_ids.shape[0]
    lane_ids = jnp.arange(expert_count, dtype=jnp.int32)
    id_onehot = (flat_ids[:, None] == lane_ids[None, :]).astype(jnp.int32)
    dest_dev = jnp.sum(id_onehot * dest_table[None, :], axis=1)
    onehot = (dest_dev[:, None] == lane_ids[None, :]).astype(jnp.int32)
    before = jnp.cumsum(onehot, axis=0) - onehot
    slot_idx = jnp.sum(before * onehot, axis=1)
    where_to = dest_dev * capacity + slot_idx
    source = (
        jnp.zeros((expert_count * capacity,), jnp.int32)
        .at[where_to]
        .set(jnp.arange(assigned, dtype=jnp.int32) + 1)
    )
    filled = (source > 0)[:, None]
    pick_idx = jnp.maximum(source - 1, 0)
    model_width = x_block.shape[1]
    x_rows = jnp.where(
        filled, jnp.take(x_block, pick_idx // 2, axis=0), jnp.zeros((), jnp.bfloat16)
    )
    g_rows = jnp.where(
        filled,
        jnp.take(g_block.reshape(assigned, model_width), pick_idx, axis=0),
        jnp.zeros((), jnp.bfloat16),
    )
    return (
        x_rows.reshape(expert_count, capacity, model_width),
        g_rows.reshape(expert_count, capacity, model_width),
        where_to,
    )


def shards(
    tokens, out_grad, gates, expert_ids, swap_list, w_in, w_out, first_moment, second_moment
):
    expert_count = lax.axis_size("expert")
    top_bit = expert_count.bit_length() - 2
    own_index = lax.axis_index("expert")
    lane_ids = jnp.arange(expert_count, dtype=jnp.int32)
    partner_me = jnp.sum(jnp.where(lane_ids == own_index, swap_list, 0))
    is_moved = partner_me != own_index
    tok_count = tokens.shape[0]
    model_width = tokens.shape[1]
    capacity = 3 * tok_count // expert_count
    grad_pair = (gates[:, :, None] * out_grad[:, None, :].astype(jnp.float32)).astype(jnp.bfloat16)
    x_buf, g_buf, where_to = pack_rows(expert_ids, tokens, grad_pair, lane_ids, capacity)
    x_recv, g_recv = (
        lax.all_to_all(x_buf, "expert", split_axis=0, concat_axis=0, tiled=True),
        lax.all_to_all(g_buf, "expert", split_axis=0, concat_axis=0, tiled=True),
    )
    x_all, g_all = (
        lax.all_gather(x_recv, "dp", axis=0, tiled=True),
        lax.all_gather(g_recv, "dp", axis=0, tiled=True),
    )
    x_rows = x_all.reshape(-1, model_width)
    g_rows = g_all.reshape(-1, model_width)
    w_in_local = w_in[0]
    w_out_local = w_out[0]
    pre_act = jnp.dot(x_rows, w_in_local, preferred_element_type=jnp.float32)
    act_grad = lax.dot_general(
        g_rows, w_out_local, (((1,), (1,)), ((), ())), preferred_element_type=jnp.float32
    )
    pre_grad = (act_grad * gelu_slope(pre_act)).astype(jnp.bfloat16)
    own_rows = lax.psum_scatter(
        lax.dot_general(
            pre_grad, w_in_local, (((1,), (1,)), ((), ())), preferred_element_type=jnp.float32
        ).astype(jnp.bfloat16),
        "dp",
        scatter_dimension=0,
        tiled=True,
    )
    returned = lax.all_to_all(
        own_rows.reshape(expert_count, capacity, model_width),
        "expert",
        split_axis=0,
        concat_axis=0,
        tiled=True,
    )
    picked = jnp.take(
        returned.reshape(expert_count * capacity, model_width), where_to, axis=0
    ).astype(jnp.float32)
    x_grad = jnp.sum(picked.reshape(tok_count, 2, model_width), axis=1).astype(jnp.bfloat16)
    weight_grad = lax.dot_general(
        x_rows, pre_grad, (((0,), (0,)), ((), ())), preferred_element_type=jnp.float32
    )
    first_new = beta_one * first_moment[0] + (1.0 - beta_one) * weight_grad
    second_new = beta_two * second_moment[0] + (1.0 - beta_two) * weight_grad * weight_grad
    adam_out = (
        first_new
        / (1.0 - beta_one**ADAM_STEP)
        / (jnp.sqrt(second_new / (1.0 - beta_two**ADAM_STEP)) + adam_eps)
    )
    adam_out = adam_out.astype(jnp.bfloat16)[None]
    swapped_step = partner(adam_out, "expert", top_bit)
    adam_out = jnp.where(is_moved, swapped_step, adam_out)
    return (x_grad, adam_out)


def solution(mesh):
    in_specs = (
        P(("dp", "expert"), None),
        P(("dp", "expert"), None),
        P(("dp", "expert"), None),
        P(("dp", "expert"), None),
        P(),
        P("expert", None, "dp"),
        P("expert", "dp", None),
        P("expert", None, "dp"),
        P("expert", None, "dp"),
    )
    out_specs = (P(("dp", "expert"), None), P("expert", None, "dp"))
    return jax.shard_map(shards, mesh=mesh, in_specs=in_specs, out_specs=out_specs, check_vma=False)
```

profile of v0, /device:TPU:17, one launch (start us, length us, event | category | flops | bytes accessed | tf_op | source)
XLA Modules:
  0.0 331.9 jit_solution(17654201795168940946)
XLA Ops:
  7.2 0.0 all-gather.5.cloned.1.call-start
  7.2 0.6 iota_add_fusion
  7.8 1.7 copy.14
  9.6 1.0 eq.46
  10.6 0.6 copy-done.1
  11.1 0.6 fusion.27
  11.7 1.3 reduce-window.6
  13.0 0.8 slice_reduce_fusion
  13.8 1.3 reduce-window.9
  15.0 0.7 slice.7
  15.7 0.8 fusion.26
  16.5 0.7 multiply_add_fusion.1
  17.1 1.6 scatter_custom_fusion
  18.7 0.6 compare_and_fusion.1
  19.3 0.6 add_maximum_fusion
  19.9 0.7 broadcast_in_dim.70
  20.6 1.4 broadcast_in_dim.72
  22.0 1.3 broadcast_in_dim.77
  23.3 0.7 pad_clamp_fusion.2
  24.0 2.3 mul.129
  26.2 3.0 mul.130
  29.2 1.4 copy.16
  30.6 1.5 mul.127
  32.2 4.6 %gather_fusion.1 = bf16[384,1152]{1,0:T(8,128)(2,1)} fusion(bf16[128,1152]{1,0:T(8,128)(2,1)} %param.9, s32[1024]{0:T(1024)S(1)} %pad_clamp_fusion.1), kind=kCustom, calls=%fused_computation.1 | custom fusion | bytes 1771008 | tf_op jit(solution)/shard_map/jit(_take)/gather | solution.py:52
  36.8 2.2 multiply_convert_fusion
  39.0 4.7 %gather_fusion = bf16[384,1152]{1,0:T(8,128)(2,1)} fusion(bf16[256,1152]{1,0:T(8,128)(2,1)} %multiply_convert_fusion, s32[1024]{0:T(1024)S(1)} %pad_clamp_fusion.2), kind=kCustom, calls=%fused_computation | custom fusion | bytes 1771008 | tf_op jit(solution)/shard_map/jit(_take)/gather | solution.py:56
  43.8 2.7 select_select_fusion.1
  46.5 27.4 %all_to_all.15 = bf16[16,24,1152]{2,1,0:T(8,128)(2,1)} all-to-all(bf16[16,24,1152]{2,1,0:T(8,128)(2,1)S(1)} %get-tuple-element.5), channel_id=1, replica_groups=mesh['dp'=2,'expert'=16] {'expert'}, dimensions={0} | all-to-all | bytes 1769472 | tf_op jit(solution)/shard_map/all_to_all | solution.py:81
  73.9 0.0 all-gather.3.cloned.1.call-start
  74.0 25.3 %all_to_all.16 = bf16[16,24,1152]{2,1,0:T(8,128)(2,1)} all-to-all(bf16[16,24,1152]{2,1,0:T(8,128)(2,1)} %get-tuple-element.4), channel_id=1, replica_groups=mesh['dp'=2,'expert'=16] {'expert'}, dimensions={0} | all-to-all | bytes 1769472 | tf_op jit(solution)/shard_map/all_to_all | solution.py:82
  99.3 0.2 reduce-scatter.2.cloned.1.call-start
  99.6 6.4 %fusion.16 = f32[768,1536]{1,0:T(8,128)} fusion(bf16[768,1152]{1,0:T(8,128)(2,1)} %bitcast.68, bf16[1,1152,1536]{2,1,0:T(8,128)(2,1)S(1)} %copy-done), kind=kOutput, calls=%fused_computation.24 | convolution fusion | flops 2717908992 | bytes 10027008 | tf_op jit(solution)/shard_map/dot_general | solution.py:92
  106.0 5.5 %all-gather.3.cloned.1.call-done = bf16[32,24,1152]{2,1,0:T(8,128)(2,1)} async-done(((bf16[16,24,1152]{2,1,0:T(8,128)(2,1)}), bf16[32,24,1152]{2,1,0:T(8,128)(2,1)}) %all-gather.3.cloned.1.call-update) | async-done | bytes 1769488 | tf_op jit(solution)/shard_map/all_gather | solution.py:86
  111.4 8.0 %fusion.13 = bf16[768,1536]{1,0:T(8,128)(2,1)S(1)} fusion(f32[768,1536]{1,0:T(8,128)} %fusion.16, bf16[768,1152]{1,0:T(8,128)(2,1)} %bitcast.70, bf16[1,1536,1152]{2,1,0:T(8,128)(2,1)} %param.15), kind=kOutput, calls=%fused_computation.21 | convolution fusion | flops 2740322304 | bytes 12386304 | tf_op jit(solution)/shard_map/dot_general | solution.py:93
  119.4 1.4 copy-done.4
  120.8 4.4 %fusion.20 = bf16[768,1152]{1,0:T(8,128)(2,1)} fusion(bf16[768,1536]{1,0:T(8,128)(2,1)S(1)} %fusion.13, bf16[1,1152,1536]{2,1,0:T(8,128)(2,1)S(1)} %copy-done), kind=kOutput, calls=%fused_computation.29 | convolution fusion | flops 2718793728 | bytes 7667712 | tf_op jit(solution)/shard_map/dot_general | solution.py:98
  125.2 15.1 %fusion.19 = bf16[1,1152,1536]{2,1,0:T(8,128)(2,1)} fusion(f32[1,1152,1536]{2,1,0:T(8,128)} %param.17, f32[1,1152,1536]{2,1,0:T(8,128)} %param.16, bf16[768,1152]{1,0:T(8,128)(2,1)} %bitcast.69, bf16[768,1536]{1,0:T(8,128)(2,1)} %copy-done.4), kind=kOutput, calls=%fused_computation.28 | convolution fusion | flops 2739142656 | bytes 21823488 | tf_op jit(solution)/shard_map/dot_general | solution.py:116
  140.3 0.8 add.90
  141.0 0.9 compare_and_fusion
  141.9 6.7 %all-to-all-start.2 = ((bf16[16,24,1152]{2,1,0:T(8,128)(2,1)}), bf16[16,24,1152]{2,1,0:T(8,128)(2,1)}, u32[]{:S(2)}, u32[]{:S(2)}) async-start(bf16[16,24,1152]{2,1,0:T(8,128)(2,1)} %bitcast.63), calls=%async_computation.3 | async-start | bytes 1769472 | tf_op jit(solution)/shard_map/all_to_all | solution.py:105
  148.6 1.3 fusion.31
  150.6 1.2 pad_clamp_fusion
  151.8 149.8 %collective-permute-done = bf16[1,1152,1536]{2,1,0:T(8,128)(2,1)} collective-permute-done((bf16[1,1152,1536]{2,1,0:T(8,128)(2,1)}, bf16[1,1152,1536]{2,1,0:T(8,128)(2,1)}, u32[]{:S(2)}, u32[]{:S(2)}) %collective-permute-start) | collective-permute-done | bytes 3538976 | tf_op jit(solution)/shard_map/ppermute | solution.py:21
  301.6 4.2 %broadcast_select_fusion = bf16[1,1152,1536]{2,1,0:T(8,128)(2,1)} fusion(bf16[1,1152,1536]{2,1,0:T(8,128)(2,1)} %collective-permute-done, bf16[1,1152,1536]{2,1,0:T(8,128)(2,1)} %fusion.19, pred[]{:T(512)S(6)} %ne.20), kind=kLoop, calls=%fused_computation.27 | loop fusion | flops 1769472 | bytes 10616833 | tf_op jit(solution)/shard_map/jit(_where)/select_n | solution.py:128
  305.8 9.9 %all-to-all-done.2 = bf16[16,24,1152]{2,1,0:T(8,128)(2,1)} async-done(((bf16[16,24,1152]{2,1,0:T(8,128)(2,1)}), bf16[16,24,1152]{2,1,0:T(8,128)(2,1)}, u32[]{:S(2)}, u32[]{:S(2)}) %all-to-all-start.2) | async-done | bytes 884768 | tf_op jit(solution)/shard_map/all_to_all | solution.py:105
  315.7 3.9 %gather_fusion.2 = bf16[256,1152]{1,0:T(8,128)(2,1)} fusion(bf16[384,1152]{1,0:T(8,128)(2,1)} %bitcast.11, s32[1024]{0:T(1024)} %pad_clamp_fusion), kind=kCustom, calls=%fused_computation.2 | custom fusion | bytes 1180672 | tf_op jit(solution)/shard_map/jit(_take)/gather | solution.py:112
  319.6 2.6 gather.23
  322.2 3.2 fusion.23
  (17 shorter events, 0.1 us)
Async XLA Ops:
  7.2 92.4 %copy-start = (bf16[1,1152,1536]{2,1,0:T(8,128)(2,1)S(1)}, bf16[1,1152,1536]{2,1,0:T(8,128)(2,1)}, u32[]{:S(2)}) copy-start(bf16[1,1152,1536]{2,1,0:T(8,128)(2,1)} %param.14) | copy-start | bytes 10616836
  7.2 92.4 %all-gather.5.cloned.1.call-start = ((), (), s32[]{:S(2)}) async-start(), calls=%async_computation.5 | async-start | bytes 2654208 | tf_op jit(solution)/shard_map/all_gather | solution.py:85
  10.6 0.6 copy-start.1
  17.1 4.8 %copy-start.3 = (s32[256,1]{0,1:T(1,128)}, s32[256,1]{0,1:T(1,128)S(1)}, u32[]{:S(2)}) copy-start(s32[256,1]{0,1:T(1,128)S(1)} %compare_select_fusion.1) | copy-start | bytes 3076
  36.8 7.0 %copy-start.2 = (pred[16,24]{1,0:T(8,128)(4,1)S(1)}, pred[16,24]{1,0:T(8,128)(4,1)}, u32[]{:S(2)}) copy-start(pred[16,24]{1,0:T(8,128)(4,1)} %broadcast_in_dim.72) | copy-start | bytes 1156
  73.9 37.5 %all-gather.3.cloned.1.call-start = ((), (), s32[]{:S(2)}) async-start(), calls=%async_computation.4 | async-start | bytes 2654208 | tf_op jit(solution)/shard_map/all_gather | solution.py:86
  99.3 42.6 %reduce-scatter.2.cloned.1.call-start = ((), (), s32[]{:S(2)}) async-start(), calls=%async_computation.6 | async-start | bytes 2654208 | tf_op jit(solution)/shard_map/reduce_scatter | solution.py:97
  119.4 1.4 copy-start.4
  140.3 161.3 %collective-permute-start = (bf16[1,1152,1536]{2,1,0:T(8,128)(2,1)}, bf16[1,1152,1536]{2,1,0:T(8,128)(2,1)}, u32[]{:S(2)}, u32[]{:S(2)}) collective-permute-start(bf16[1,1152,1536]{2,1,0:T(8,128)(2,1)} %fusion.19), channel_id=1, source_target_pairs={{0,8},{8,0},{1,9},{9,1},{2,10},{10,2},{3,11},{11,3},{4,12},{12,4},... | collective-permute-start | bytes 10616840 | tf_op jit(solution)/shard_map/ppermute | solution.py:21
  141.9 173.7 %all-to-all-start.2 = ((bf16[16,24,1152]{2,1,0:T(8,128)(2,1)}), bf16[16,24,1152]{2,1,0:T(8,128)(2,1)}, u32[]{:S(2)}, u32[]{:S(2)}) async-start(bf16[16,24,1152]{2,1,0:T(8,128)(2,1)} %bitcast.63), calls=%async_computation.3 | async-start | bytes 1769472 | tf_op jit(solution)/shard_map/all_to_all | solution.py:105
Sparse Core Ops, SparseCore 0:
  74.1 11.0 all-gather.4
  99.5 11.9 all-gather.2
  125.3 10.4 reduce-scatter.1
where the time goes:
time: 333 us; the launch traced here: 332 us
  waiting for transfers between devices  165 us (50%)
  blocking collectives  52.8 us (16%)
  local copies, waits for them, and re-layouts  35.9 us (11%)
  matrix products  33.7 us (10%)
  other arithmetic  22.7 us (7%)
  between operations  14.5 us (4%)
  starting transfers between devices  7.01 us (2%)
    ppermute x1, waiting for transfers between devices, partner(): return lax.ppermute(block, axis, route)  150 us
    all_to_all x1, blocking collectives, shards(): lax.all_to_all(x_buf, 'expert', split_axis=0, concat_axis=0, tiled=True)  27.4 us
    all_to_all x1, blocking collectives, shards(): lax.all_to_all(g_buf, 'expert', split_axis=0, concat_axis=0, tiled=True)  25.3 us
    dot_general x1, matrix products, shards(): lax.dot_general(x_rows, pre_grad, (((0,), (0,)), ((), ())), preferred_ele...  15.1 us
    all_to_all x1, waiting for transfers between devices, shards(): lax.all_to_all(own_rows.reshape(expert_count, capacity, model_width), 'ex...  9.91 us
    dot_general x1, matrix products, shards(): lax.dot_general(g_rows, w_out_local, (((1,), (1,)), ((), ())), preferred_...  7.95 us
    mul x3, local copies, waits for them, and re-layouts, shards(): gates[:, :, None] * out_grad[:, None, :].astype(jnp.float32)  6.8 us
    all_to_all x1, starting transfers between devices, shards(): lax.all_to_all(own_rows.reshape(expert_count, capacity, model_width), 'ex...  6.7 us
  transfers between devices with their start and end apart: 5, of which 3 were waited for; matrix products, arithmetic and copies ran while one was open for 9% of the time, Pallas kernels for 0%

commit v1 on v0

--- a/solution.py
+++ b/solution.py
@@ -2,6 +2,7 @@
 import jax.numpy as jnp
 from jax import lax
 from jax.sharding import PartitionSpec as P
+from jax.lax import axis_index, ppermute, psum
 
 ADAM_STEP = 100
 coef_c = 0.7978845608028654
@@ -9,6 +10,18 @@
 beta_one = 0.9
 beta_two = 0.999
 adam_eps = 1e-08
+
+
+def close_the_strips_all(patch, in_dim, inp):
+    outer = patch.shape
+    opened = patch.reshape(*outer[:in_dim], inp, outer[in_dim] // inp, *outer[in_dim + 1 :])
+    return jnp.moveaxis(opened, in_dim, 0)
+
+
+def _wait_routes_all(m, at_axis):
+    part_now = list(m.shape[1:])
+    part_now[at_axis] *= m.shape[0]
+    return jnp.moveaxis(m, 0, at_axis).reshape(part_now)
 
 
 def partner(block, axis, apart):
@@ -66,6 +79,21 @@
 def shards(
     tokens, out_grad, gates, expert_ids, swap_list, w_in, w_out, first_moment, second_moment
 ):
+
+    def launch_shapes_up(raw, chip_axis, local_array, load):
+        work_now = psum(1, axis_name=chip_axis)
+        a_now, current_value = (work_now, axis_index(chip_axis))
+        fresh = close_the_strips_all(raw, local_array, a_now)
+        buffers = [fresh[current_value]]
+        for i0 in [*range(1, a_now)]:
+            k_now = fresh[current_value ^ i0]
+            buffers.append(
+                ppermute(k_now, axis_name=chip_axis, perm=[(k0, k0 ^ i0) for k0 in range(a_now)])
+            )
+        v_next = jnp.stack(buffers)
+        fresh = v_next[current_value ^ jnp.arange(a_now)]
+        return _wait_routes_all(fresh, load)
+
     expert_count = lax.axis_size("expert")
     top_bit = expert_count.bit_length() - 2
     own_index = lax.axis_index("expert")
@@ -79,7 +107,7 @@
     x_buf, g_buf, where_to = pack_rows(expert_ids, tokens, grad_pair, lane_ids, capacity)
     x_recv, g_recv = (
         lax.all_to_all(x_buf, "expert", split_axis=0, concat_axis=0, tiled=True),
-        lax.all_to_all(g_buf, "expert", split_axis=0, concat_axis=0, tiled=True),
+        launch_shapes_up(g_buf, "expert", 0, 0),
     )
     x_all, g_all = (
         lax.all_gather(x_recv, "dp", axis=0, tiled=True),

time: 333 us -> 344 us (1.033)
  blocking collectives: 52.8 us -> 0 us
  starting transfers between devices: 7.01 us -> 29.6 us
  waiting for transfers between devices: 165 us -> 185 us
  local copies, waits for them, and re-layouts: 35.9 us -> 55 us
    all_to_all x2 -> x0, blocking collectives: 52.8 us -> none  [the longest x1 27.4 us: shards(): lax.all_to_all(x_buf, 'expert', split_axis=0, concat_axis=0, tiled=True)]
    ppermute x0 -> x15, starting transfers between devices: none -> 17 us  [launch_shapes_up(): ppermute(k_now, axis_name=chip_axis, perm=[(k0, k0 ^ i0) for k0 in range(...]
    unnamed x12 -> x24, local copies, waits for them, and re-layouts: 5.13 us -> 20.3 us
    ppermute x0 -> x15, waiting for transfers between devices: none -> 12.7 us  [launch_shapes_up(): ppermute(k_now, axis_name=chip_axis, perm=[(k0, k0 ^ i0) for k0 in range(...]
    all_gather x1, waiting for transfers between devices: 0.02 us -> 5.83 us  [shards(): lax.all_gather(x_recv, 'dp', axis=0, tiled=True)]
    all_to_all x0 -> x1, starting transfers between devices: none -> 5.62 us  [shards(): lax.all_to_all(x_buf, 'expert', split_axis=0, concat_axis=0, tiled=True)]
  transfers between devices with their start and end apart: 5 -> 21, of which waited for: 3 -> 11; matrix products, arithmetic and copies ran while one was open for 9% -> 17% of each run, Pallas kernels for 0% -> 0%
where the time goes in v1:
time: 344 us; the launch traced here: 342 us
  waiting for transfers between devices  185 us (54%)
  local copies, waits for them, and re-layouts  55 us (16%)
  matrix products  33.8 us (10%)
  starting transfers between devices  29.6 us (9%)
  other arithmetic  23.7 us (7%)
  between operations  14.6 us (4%)
    ppermute x1, waiting for transfers between devices, partner(): return lax.ppermute(block, axis, route)  150 us
    unnamed x24, local copies, waits for them, and re-layouts  20.3 us
    ppermute x15, starting transfers between devices, launch_shapes_up(): ppermute(k_now, axis_name=chip_axis, perm=[(k0, k0 ^ i0) for k0 in range(...  17 us
    dot_general x1, matrix products, shards(): lax.dot_general(x_rows, pre_grad, (((0,), (0,)), ((), ())), preferred_ele...  15.1 us
    ppermute x15, waiting for transfers between devices, launch_shapes_up(): ppermute(k_now, axis_name=chip_axis, perm=[(k0, k0 ^ i0) for k0 in range(...  12.7 us
    all_to_all x1, waiting for transfers between devices, shards(): lax.all_to_all(own_rows.reshape(expert_count, capacity, model_width), 'ex...  9.92 us
    dot_general x1, matrix products, shards(): lax.dot_general(g_rows, w_out_local, (((1,), (1,)), ((), ())), preferred_...  7.95 us
    all_gather x1, waiting for transfers between devices, shards(): lax.all_gather(g_recv, 'dp', axis=0, tiled=True)  7 us
  transfers between devices with their start and end apart: 21, of which 11 were waited for; matrix products, arithmetic and copies ran while one was open for 17% of the time, Pallas kernels for 0%

profile of v1, /device:TPU:17, one launch (start us, length us, event | category | flops | bytes accessed | tf_op | source)
XLA Modules:
  0.0 342.1 jit_solution(1412385676071341798)
XLA Ops:
  7.8 1.7 copy.14
  11.7 1.3 reduce-window.6
  13.7 1.3 reduce-window.9
  17.1 1.6 scatter_custom_fusion
  19.9 2.3 mul.129
  22.1 3.0 mul.130
  25.1 1.4 copy.16
  26.6 1.5 mul.127
  30.2 2.2 multiply_convert_fusion
  32.5 4.7 %gather_fusion = bf16[384,1152]{1,0:T(8,128)(2,1)} fusion(bf16[256,1152]{1,0:T(8,128)(2,1)} %multiply_convert_fusion, s32[1024]{0:T(1024)S(1)} %get-tuple-element.23), kind=kCustom, calls=%fused_computation | custom fusion | bytes 1771008 | tf_op jit(solution)/shard_map/jit(_take)/gather | solution.py:69
  37.2 1.4 select_select_fusion.1
  40.8 1.2 collective-permute-start.1
  42.3 1.3 collective-permute-start.3
  45.4 4.6 %gather_fusion.2 = bf16[384,1152]{1,0:T(8,128)(2,1)} fusion(bf16[128,1152]{1,0:T(8,128)(2,1)} %param.9, s32[1024]{0:T(1024)S(1)} %get-tuple-element.22), kind=kCustom, calls=%fused_computation.2 | custom fusion | bytes 1771008 | tf_op jit(solution)/shard_map/jit(_take)/gather | solution.py:65
  50.0 2.3 select_select_fusion
  52.3 5.6 %all-to-all-start = ((bf16[16,24,1152]{2,1,0:T(8,128)(2,1)}), bf16[16,24,1152]{2,1,0:T(8,128)(2,1)}, u32[]{:S(2)}, u32[]{:S(2)}) async-start(bf16[16,24,1152]{2,1,0:T(8,128)(2,1)} %select_select_fusion), calls=%async_computation | async-start | bytes 1769472 | tf_op jit(solution)/shard_map/all_to_all | solution.py:109
  58.0 2.1 collective-permute-start.5
  60.1 1.4 bitcast_dynamic-update-slice_fusion.14
  62.7 1.4 bitcast_dynamic-update-slice_fusion.13
  64.5 1.4 bitcast_dynamic-update-slice_fusion.12
  65.9 2.1 collective-permute-start.8
  68.0 1.4 bitcast_dynamic-update-slice_fusion.11
  70.6 1.4 bitcast_dynamic-update-slice_fusion.10
  72.1 2.3 collective-permute-done.5
  77.1 5.6 %collective-permute-done.7 = bf16[1,24,1152]{2,1,0:T(8,128)(2,1)S(1)} collective-permute-done((bf16[1,24,1152]{2,1,0:T(8,128)(2,1)}, bf16[1,24,1152]{2,1,0:T(8,128)(2,1)S(1)}, u32[]{:S(2)}, u32[]{:S(2)}) %collective-permute-start.7) | collective-permute-done | bytes 55328 | tf_op jit(solution)/shard_map/ppermute | solution.py:91
  84.4 2.7 collective-permute-start.13
  90.0 1.4 bitcast_dynamic-update-slice_fusion.3
  91.7 1.4 bitcast_dynamic-update-slice_fusion.2
  93.1 1.9 collective-permute-done.13
  95.0 1.4 bitcast_dynamic-update-slice_fusion.1
  96.4 1.5 collective-permute-done.14
  98.0 1.4 bitcast_dynamic-update-slice_fusion
  99.4 2.7 gather_fusion.1
  102.4 5.8 %all-gather.4.cloned.1.call-done = bf16[32,24,1152]{2,1,0:T(8,128)(2,1)} async-done(((bf16[16,24,1152]{2,1,0:T(8,128)(2,1)}), bf16[32,24,1152]{2,1,0:T(8,128)(2,1)}) %all-gather.4.cloned.1.call-update) | async-done | bytes 1769488 | tf_op jit(solution)/shard_map/all_gather | solution.py:113
  108.2 6.4 %fusion.16 = f32[768,1536]{1,0:T(8,128)} fusion(bf16[768,1152]{1,0:T(8,128)(2,1)} %bitcast.132, bf16[1,1152,1536]{2,1,0:T(8,128)(2,1)S(1)} %copy-done), kind=kOutput, calls=%fused_computation.25 | convolution fusion | flops 2717908992 | bytes 10027008 | tf_op jit(solution)/shard_map/dot_general | solution.py:120
  114.6 7.0 %all-gather.6.cloned.1.call-done = bf16[32,24,1152]{2,1,0:T(8,128)(2,1)} async-done(((bf16[16,24,1152]{2,1,0:T(8,128)(2,1)}), bf16[32,24,1152]{2,1,0:T(8,128)(2,1)}) %all-gather.6.cloned.1.call-update) | async-done | bytes 1769488 | tf_op jit(solution)/shard_map/all_gather | solution.py:114
  121.6 7.9 %fusion.13 = bf16[768,1536]{1,0:T(8,128)(2,1)S(1)} fusion(f32[768,1536]{1,0:T(8,128)} %fusion.16, bf16[768,1152]{1,0:T(8,128)(2,1)} %bitcast.134, bf16[1,1536,1152]{2,1,0:T(8,128)(2,1)} %param.15), kind=kOutput, calls=%fused_computation.22 | convolution fusion | flops 2740322304 | bytes 12386304 | tf_op jit(solution)/shard_map/dot_general | solution.py:121
  129.6 1.4 copy-done.3
  131.0 4.4 %fusion.20 = bf16[768,1152]{1,0:T(8,128)(2,1)} fusion(bf16[768,1536]{1,0:T(8,128)(2,1)S(1)} %fusion.13, bf16[1,1152,1536]{2,1,0:T(8,128)(2,1)S(1)} %copy-done), kind=kOutput, calls=%fused_computation.30 | convolution fusion | flops 2718793728 | bytes 7667712 | tf_op jit(solution)/shard_map/dot_general | solution.py:126
  135.4 15.1 %fusion.19 = bf16[1,1152,1536]{2,1,0:T(8,128)(2,1)} fusion(f32[1,1152,1536]{2,1,0:T(8,128)} %param.17, f32[1,1152,1536]{2,1,0:T(8,128)} %param.16, bf16[768,1152]{1,0:T(8,128)(2,1)} %bitcast.133, bf16[768,1536]{1,0:T(8,128)(2,1)} %copy-done.3), kind=kOutput, calls=%fused_computation.29 | convolution fusion | flops 2739142656 | bytes 21823488 | tf_op jit(solution)/shard_map/dot_general | solution.py:144
  152.1 6.7 %all-to-all-start.1 = ((bf16[16,24,1152]{2,1,0:T(8,128)(2,1)}), bf16[16,24,1152]{2,1,0:T(8,128)(2,1)}, u32[]{:S(2)}, u32[]{:S(2)}) async-start(bf16[16,24,1152]{2,1,0:T(8,128)(2,1)} %bitcast.127), calls=%async_computation.2 | async-start | bytes 1769472 | tf_op jit(solution)/shard_map/all_to_all | solution.py:133
  158.8 1.3 fusion.31
  162.0 149.8 %collective-permute-done.15 = bf16[1,1152,1536]{2,1,0:T(8,128)(2,1)} collective-permute-done((bf16[1,1152,1536]{2,1,0:T(8,128)(2,1)}, bf16[1,1152,1536]{2,1,0:T(8,128)(2,1)}, u32[]{:S(2)}, u32[]{:S(2)}) %collective-permute-start.15) | collective-permute-done | bytes 3538976 | tf_op jit(solution)/shard_map/ppermute | solution.py:34
  311.8 4.2 %broadcast_select_fusion = bf16[1,1152,1536]{2,1,0:T(8,128)(2,1)} fusion(bf16[1,1152,1536]{2,1,0:T(8,128)(2,1)} %collective-permute-done.15, bf16[1,1152,1536]{2,1,0:T(8,128)(2,1)} %fusion.19, pred[]{:T(512)S(6)} %ne.20), kind=kLoop, calls=%fused_computation.28 | loop fusion | flops 1769472 | bytes 10616833 | tf_op jit(solution)/shard_map/jit(_where)/select_n | solution.py:156
  316.0 9.9 %all-to-all-done.1 = bf16[16,24,1152]{2,1,0:T(8,128)(2,1)} async-done(((bf16[16,24,1152]{2,1,0:T(8,128)(2,1)}), bf16[16,24,1152]{2,1,0:T(8,128)(2,1)}, u32[]{:S(2)}, u32[]{:S(2)}) %all-to-all-start.1) | async-done | bytes 884768 | tf_op jit(solution)/shard_map/all_to_all | solution.py:133
  325.9 3.9 %gather_fusion.3 = bf16[256,1152]{1,0:T(8,128)(2,1)} fusion(bf16[384,1152]{1,0:T(8,128)(2,1)} %bitcast.43, s32[1024]{0:T(1024)} %pad_clamp_fusion), kind=kCustom, calls=%fused_computation.3 | custom fusion | bytes 1180672 | tf_op jit(solution)/shard_map/jit(_take)/gather | solution.py:140
  329.8 2.6 gather.27
  332.4 3.2 fusion.23
  (64 shorter events, 26.4 us)
Async XLA Ops:
  7.2 101.1 %copy-start = (bf16[1,1152,1536]{2,1,0:T(8,128)(2,1)S(1)}, bf16[1,1152,1536]{2,1,0:T(8,128)(2,1)}, u32[]{:S(2)}) copy-start(bf16[1,1152,1536]{2,1,0:T(8,128)(2,1)} %param.14) | copy-start | bytes 10616836
  10.5 0.6 copy-start.1
  17.1 12.4 %copy-start.2 = (s32[256,1]{0,1:T(1,128)}, s32[256,1]{0,1:T(1,128)S(1)}, u32[]{:S(2)}) copy-start(s32[256,1]{0,1:T(1,128)S(1)} %compare_select_fusion.1) | copy-start | bytes 3076
  39.6 18.4 %collective-permute-start = (bf16[1,24,1152]{2,1,0:T(8,128)(2,1)}, bf16[1,24,1152]{2,1,0:T(8,128)(2,1)}, u32[]{:S(2)}, u32[]{:S(2)}) collective-permute-start(bf16[1,24,1152]{2,1,0:T(8,128)(2,1)} %get-tuple-element.18), channel_id=1, source_target_pairs={{0,1},{1,0},{2,3},{3,2},{4,5},{5,4},{6,7},{7,6},{8,9},{9,8},{10,11... | collective-permute-start | bytes 165896 | tf_op jit(solution)/shard_map/ppermute | solution.py:91
  40.8 20.7 %collective-permute-start.1 = (bf16[1,24,1152]{2,1,0:T(8,128)(2,1)}, bf16[1,24,1152]{2,1,0:T(8,128)(2,1)}, u32[]{:S(2)}, u32[]{:S(2)}) collective-permute-start(bf16[1,24,1152]{2,1,0:T(8,128)(2,1)} %get-tuple-element.17), channel_id=1, source_target_pairs={{0,2},{1,3},{2,0},{3,1},{4,6},{5,7},{6,4},{7,5},{8,10},{9,11},{10,... | collective-permute-start | bytes 165896 | tf_op jit(solution)/shard_map/ppermute | solution.py:91
  42.1 22.1 %collective-permute-start.2 = (bf16[1,24,1152]{2,1,0:T(8,128)(2,1)}, bf16[1,24,1152]{2,1,0:T(8,128)(2,1)}, u32[]{:S(2)}, u32[]{:S(2)}) collective-permute-start(bf16[1,24,1152]{2,1,0:T(8,128)(2,1)} %get-tuple-element.16), channel_id=1, source_target_pairs={{0,3},{1,2},{2,1},{3,0},{4,7},{5,6},{6,5},{7,4},{8,11},{9,10},{10,... | collective-permute-start | bytes 165896 | tf_op jit(solution)/shard_map/ppermute | solution.py:91
  42.3 23.6 %collective-permute-start.3 = (bf16[1,24,1152]{2,1,0:T(8,128)(2,1)}, bf16[1,24,1152]{2,1,0:T(8,128)(2,1)}, u32[]{:S(2)}, u32[]{:S(2)}) collective-permute-start(bf16[1,24,1152]{2,1,0:T(8,128)(2,1)} %get-tuple-element.15), channel_id=1, source_target_pairs={{0,4},{1,5},{2,6},{3,7},{4,0},{5,1},{6,2},{7,3},{8,12},{9,13},{10,... | collective-permute-start | bytes 165896 | tf_op jit(solution)/shard_map/ppermute | solution.py:91
  43.6 25.9 %collective-permute-start.4 = (bf16[1,24,1152]{2,1,0:T(8,128)(2,1)}, bf16[1,24,1152]{2,1,0:T(8,128)(2,1)}, u32[]{:S(2)}, u32[]{:S(2)}) collective-permute-start(bf16[1,24,1152]{2,1,0:T(8,128)(2,1)} %get-tuple-element.14), channel_id=1, source_target_pairs={{0,5},{1,4},{2,7},{3,6},{4,1},{5,0},{6,3},{7,2},{8,13},{9,12},{10,... | collective-permute-start | bytes 165896 | tf_op jit(solution)/shard_map/ppermute | solution.py:91
  52.3 37.6 %all-to-all-start = ((bf16[16,24,1152]{2,1,0:T(8,128)(2,1)}), bf16[16,24,1152]{2,1,0:T(8,128)(2,1)}, u32[]{:S(2)}, u32[]{:S(2)}) async-start(bf16[16,24,1152]{2,1,0:T(8,128)(2,1)} %select_select_fusion), calls=%async_computation | async-start | bytes 1769472 | tf_op jit(solution)/shard_map/all_to_all | solution.py:109
  57.9 50.3 %all-gather.4.cloned.1.call-start = ((), (), s32[]{:S(2)}) async-start(), calls=%async_computation.3 | async-start | bytes 2654208 | tf_op jit(solution)/shard_map/all_gather | solution.py:113
  58.0 16.4 %collective-permute-start.5 = (bf16[1,24,1152]{2,1,0:T(8,128)(2,1)}, bf16[1,24,1152]{2,1,0:T(8,128)(2,1)S(1)}, u32[]{:S(2)}, u32[]{:S(2)}) collective-permute-start(bf16[1,24,1152]{2,1,0:T(8,128)(2,1)} %get-tuple-element.13), channel_id=1, source_target_pairs={{0,6},{1,7},{2,4},{3,5},{4,2},{5,3},{6,0},{7,1},{8,14},{9,15},{10,... | collective-permute-start | bytes 165896 | tf_op jit(solution)/shard_map/ppermute | solution.py:91
  61.6 14.9 %collective-permute-start.6 = (bf16[1,24,1152]{2,1,0:T(8,128)(2,1)}, bf16[1,24,1152]{2,1,0:T(8,128)(2,1)S(1)}, u32[]{:S(2)}, u32[]{:S(2)}) collective-permute-start(bf16[1,24,1152]{2,1,0:T(8,128)(2,1)} %get-tuple-element.12), channel_id=1, source_target_pairs={{0,7},{1,6},{2,5},{3,4},{4,3},{5,2},{6,1},{7,0},{8,15},{9,14},{10,... | collective-permute-start | bytes 165896 | tf_op jit(solution)/shard_map/ppermute | solution.py:91
  64.2 18.5 %collective-permute-start.7 = (bf16[1,24,1152]{2,1,0:T(8,128)(2,1)}, bf16[1,24,1152]{2,1,0:T(8,128)(2,1)S(1)}, u32[]{:S(2)}, u32[]{:S(2)}) collective-permute-start(bf16[1,24,1152]{2,1,0:T(8,128)(2,1)} %get-tuple-element.11), channel_id=1, source_target_pairs={{0,8},{1,9},{2,10},{3,11},{4,12},{5,13},{6,14},{7,15},{8,0},{9,1},... | collective-permute-start | bytes 165896 | tf_op jit(solution)/shard_map/ppermute | solution.py:91
  65.9 18.5 %collective-permute-start.8 = (bf16[1,24,1152]{2,1,0:T(8,128)(2,1)}, bf16[1,24,1152]{2,1,0:T(8,128)(2,1)S(1)}, u32[]{:S(2)}, u32[]{:S(2)}) collective-permute-start(bf16[1,24,1152]{2,1,0:T(8,128)(2,1)} %get-tuple-element.10), channel_id=1, source_target_pairs={{0,9},{1,8},{2,11},{3,10},{4,13},{5,12},{6,15},{7,14},{8,1},{9,0},... | collective-permute-start | bytes 165896 | tf_op jit(solution)/shard_map/ppermute | solution.py:91
  69.4 18.3 %collective-permute-start.9 = (bf16[1,24,1152]{2,1,0:T(8,128)(2,1)}, bf16[1,24,1152]{2,1,0:T(8,128)(2,1)S(1)}, u32[]{:S(2)}, u32[]{:S(2)}) collective-permute-start(bf16[1,24,1152]{2,1,0:T(8,128)(2,1)} %get-tuple-element.9), channel_id=1, source_target_pairs={{0,10},{1,11},{2,8},{3,9},{4,14},{5,15},{6,12},{7,13},{8,2},{9,3},... | collective-permute-start | bytes 165896 | tf_op jit(solution)/shard_map/ppermute | solution.py:91
  74.4 14.8 %collective-permute-start.10 = (bf16[1,24,1152]{2,1,0:T(8,128)(2,1)}, bf16[1,24,1152]{2,1,0:T(8,128)(2,1)S(1)}, u32[]{:S(2)}, u32[]{:S(2)}) collective-permute-start(bf16[1,24,1152]{2,1,0:T(8,128)(2,1)} %get-tuple-element.8), channel_id=1, source_target_pairs={{0,11},{1,10},{2,9},{3,8},{4,15},{5,14},{6,13},{7,12},{8,3},{9,2},... | collective-permute-start | bytes 165896 | tf_op jit(solution)/shard_map/ppermute | solution.py:91
  76.5 13.5 %collective-permute-start.11 = (bf16[1,24,1152]{2,1,0:T(8,128)(2,1)}, bf16[1,24,1152]{2,1,0:T(8,128)(2,1)}, u32[]{:S(2)}, u32[]{:S(2)}) collective-permute-start(bf16[1,24,1152]{2,1,0:T(8,128)(2,1)} %get-tuple-element.7), channel_id=1, source_target_pairs={{0,12},{1,13},{2,14},{3,15},{4,8},{5,9},{6,10},{7,11},{8,4},{9,5},... | collective-permute-start | bytes 165896 | tf_op jit(solution)/shard_map/ppermute | solution.py:91
  82.7 9.0 %collective-permute-start.12 = (bf16[1,24,1152]{2,1,0:T(8,128)(2,1)}, bf16[1,24,1152]{2,1,0:T(8,128)(2,1)}, u32[]{:S(2)}, u32[]{:S(2)}) collective-permute-start(bf16[1,24,1152]{2,1,0:T(8,128)(2,1)} %get-tuple-element.6), channel_id=1, source_target_pairs={{0,13},{1,12},{2,15},{3,14},{4,9},{5,8},{6,11},{7,10},{8,5},{9,4},... | collective-permute-start | bytes 165896 | tf_op jit(solution)/shard_map/ppermute | solution.py:91
  84.4 10.6 %collective-permute-start.13 = (bf16[1,24,1152]{2,1,0:T(8,128)(2,1)}, bf16[1,24,1152]{2,1,0:T(8,128)(2,1)}, u32[]{:S(2)}, u32[]{:S(2)}) collective-permute-start(bf16[1,24,1152]{2,1,0:T(8,128)(2,1)} %get-tuple-element.5), channel_id=1, source_target_pairs={{0,14},{1,15},{2,12},{3,13},{4,10},{5,11},{6,8},{7,9},{8,6},{9,7},... | collective-permute-start | bytes 165896 | tf_op jit(solution)/shard_map/ppermute | solution.py:91
  87.8 10.2 %collective-permute-start.14 = (bf16[1,24,1152]{2,1,0:T(8,128)(2,1)}, bf16[1,24,1152]{2,1,0:T(8,128)(2,1)}, u32[]{:S(2)}, u32[]{:S(2)}) collective-permute-start(bf16[1,24,1152]{2,1,0:T(8,128)(2,1)} %get-tuple-element.4), channel_id=1, source_target_pairs={{0,15},{1,14},{2,13},{3,12},{4,11},{5,10},{6,9},{7,8},{8,7},{9,6},... | collective-permute-start | bytes 165896 | tf_op jit(solution)/shard_map/ppermute | solution.py:91
  89.9 31.7 %all-gather.6.cloned.1.call-start = ((), (), s32[]{:S(2)}) async-start(), calls=%async_computation.5 | async-start | bytes 2654208 | tf_op jit(solution)/shard_map/all_gather | solution.py:114
  102.1 50.0 %reduce-scatter.2.cloned.1.call-start = ((), (), s32[]{:S(2)}) async-start(), calls=%async_computation.4 | async-start | bytes 2654208 | tf_op jit(solution)/shard_map/reduce_scatter | solution.py:125
  129.6 1.4 copy-start.3
  150.5 161.3 %collective-permute-start.15 = (bf16[1,1152,1536]{2,1,0:T(8,128)(2,1)}, bf16[1,1152,1536]{2,1,0:T(8,128)(2,1)}, u32[]{:S(2)}, u32[]{:S(2)}) collective-permute-start(bf16[1,1152,1536]{2,1,0:T(8,128)(2,1)} %fusion.19), channel_id=1, source_target_pairs={{0,8},{8,0},{1,9},{9,1},{2,10},{10,2},{3,11},{11,3},{4,12},{12,4},... | collective-permute-start | bytes 10616840 | tf_op jit(solution)/shard_map/ppermute | solution.py:34
  152.1 173.8 %all-to-all-start.1 = ((bf16[16,24,1152]{2,1,0:T(8,128)(2,1)}), bf16[16,24,1152]{2,1,0:T(8,128)(2,1)}, u32[]{:S(2)}, u32[]{:S(2)}) async-start(bf16[16,24,1152]{2,1,0:T(8,128)(2,1)} %bitcast.127), calls=%async_computation.2 | async-start | bytes 1769472 | tf_op jit(solution)/shard_map/all_to_all | solution.py:133
Sparse Core Ops, SparseCore 0:
  90.0 18.1 all-gather.3
  110.3 11.2 all-gather.5
  135.5 10.4 reduce-scatter.1
